TPU v7x, 32 devices: a whole 2x2x4 slice. The times are simulated.
32 devices in a mesh: rep: 4 (over y, core), shard: 8 (over z, x).
Axes of the slice: x: 2, y: 2, z: 4, core: 2. Of those that a mesh axis runs over, the one named last changes fastest.
Arguments:
- grad_kv: bfloat16 [4, 2, 8192, 1024], P('rep', None, 'shard'), may hold values from -24 to 24
- error_kv: float32 [4, 2, 8192, 1024], P('rep', None, 'shard'), may hold values from -12 to 12
- basis_kv: float32 [2, 1024, 64], replicated, may hold values from -6 to 6
Outputs:
- update_kv: bfloat16 [2, 8192, 1024], P(None, 'shard')
- new_error: float32 [4, 2, 8192, 1024], P('rep', None, 'shard')
- basis_next: float32 [2, 1024, 64], replicated
All inputs are finite; a program needn't handle non-finite values.
Results may differ from a plain program's by a relative error of at most 0.001.
Values sent between devices are 32-bit elements; how exact they have to be, the bound alone decides.
No kernel may reach another device: no remote copies, remote signals or barrier semaphores. Data moves between devices by JAX's collectives and lax.ppermute only.
A program may use at most 64 MiB of HBM per device.

v0:
```python
import jax
import jax.numpy as jnp
from jax import lax
from jax.sharding import PartitionSpec as P


def orthogonal(left, gram):
    chol = jnp.linalg.cholesky(gram)
    ortho = lax.linalg.triangular_solve(chol, left, left_side=False, lower=True, transpose_a=True)
    return (chol, ortho)


def on_device(grad_kv, error_kv, basis_kv):
    highest = lax.Precision.HIGHEST
    replicas = lax.axis_size("rep")
    merged = grad_kv[0].astype(jnp.float32) + error_kv[0]
    local_left = jnp.einsum("mrc,mck->mrk", merged, basis_kv, precision=highest)
    left = lax.psum(local_left, "rep") / replicas
    local_gram = jnp.einsum("mrk,mrl->mkl", left, left, precision=highest)
    gram = lax.psum(local_gram, "shard")
    chol, ortho = orthogonal(left, gram)
    local_right = jnp.einsum("mrc,mrk->mck", merged, ortho, precision=highest)
    shares = lax.psum_scatter(local_right, "shard", scatter_dimension=1, tiled=True)
    shares = lax.psum(shares, "rep")
    right = lax.all_gather(shares, "shard", axis=1, tiled=True) / replicas
    approx = jnp.einsum("mrk,mck->mrc", ortho, right, precision=highest)
    new_error = (merged - approx)[None]
    return (approx.astype(jnp.bfloat16), new_error, right)


def solution(mesh):
    placed = (P("rep", None, "shard", None), P("rep", None, "shard", None), P())
    return jax.shard_map(
        on_device,
        mesh=mesh,
        in_specs=placed,
        out_specs=(P(None, "shard", None), P("rep", None, "shard", None), P()),
        check_vma=False,
    )
```

profile of v0, /device:TPU:0, one launch (start us, length us, event | category | flops | bytes accessed | tf_op | source)
XLA Modules:
  0.0 273.9 jit_solution(2722910858909565346)
XLA Ops:
  7.2 0.0 copy-start
  7.2 0.0 all-reduce.3.cloned.1.call-start
  7.2 1.0 copy-done
  8.2 12.4 %fusion.2 = f32[2,1024,64]{1,2,0:T(8,128)} fusion(f32[2,1024,64]{1,2,0:T(8,128)S(1)} %copy-done, f32[1,2,1024,1024]{3,2,1,0:T(8,128)} %param.4, bf16[1,2,1024,1024]{3,2,1,0:T(8,128)(2,1)} %param.3), kind=kOutput, calls=%fused_computation.3 | convolution fusion | flops 1614807040 | bytes 13631488 | tf_op jit(solution)/shard_map/mrc,mck->mrk/dot_general | solution.py:17
  20.6 0.0 all-reduce.3.cloned.1.call-update
  20.6 0.0 reduce-scatter.2.cloned.1.call-start
  20.7 36.2 %all-reduce.3.cloned.1.call-done = f32[2,1024,64]{1,2,0:T(8,128)} async-done(((f32[2,1024,64]{1,2,0:T(8,128)}), f32[2,1024,64]{1,2,0:T(8,128)}) %all-reduce.3.cloned.1.call-update) | async-done | bytes 524304 | tf_op jit(solution)/shard_map/psum | solution.py:18
  56.9 1.9 fusion.7
  58.8 37.5 %psum.22 = f32[2,64,64]{1,2,0:T(8,128)S(1)} all-reduce(f32[2,64,64]{1,2,0:T(8,128)S(1)} %fusion.7), channel_id=1, replica_groups=mesh['rep'=4,'shard'=8] {'shard'}, use_global_device_ids=true, to_apply=%region_1.0 | all-reduce | flops 8192 | bytes 65536 | tf_op jit(solution)/shard_map/psum | solution.py:20
  96.3 0.1 copy.10
  96.4 11.7 %custom-call.7 = f32[2,64,64]{2,1,0:T(8,128)S(1)} custom-call(f32[2,64,64]{2,1,0:T(8,128)S(1)} %fusion.12), custom_call_target="Cholesky" | custom-call | tf_op jit(solution)/shard_map/jit(cholesky)/cholesky | solution.py:8
  108.2 0.1 compare_reduce_fusion
  108.3 0.1 select_bitcast_fusion
  108.4 9.8 %custom-call.8 = f32[2,1,64,64]{2,3,1,0:T(8,128)S(1)} custom-call(f32[2,1,64,64]{3,2,1,0:T(8,128)S(1)} %select_bitcast_fusion), custom_call_target="InvertDiagBlocksLowerTriangular" | custom-call | tf_op jit(solution)/shard_map/triangular_solve | solution.py:9
  118.2 1.7 fusion.5
  119.9 9.6 %fusion = f32[2,1024,64]{1,2,0:T(8,128)} fusion(f32[2,1024,64]{1,2,0:T(8,128)S(1)} %fusion.5, f32[1,2,1024,1024]{3,2,1,0:T(8,128)} %param.4, bf16[1,2,1024,1024]{3,2,1,0:T(8,128)(2,1)} %param.3), kind=kOutput, calls=%fused_computation.1 | convolution fusion | flops 1614807040 | bytes 13631488 | tf_op jit(solution)/shard_map/mrc,mrk->mck/dot_general | solution.py:22
  129.6 0.0 reduce-scatter.2.cloned.1.call-update
  129.6 0.0 all-reduce.5.cloned.1.call-start
  129.6 59.7 %reduce-scatter.2.cloned.1.call-done = f32[2,128,64]{1,2,0:T(8,128)} async-done(((f32[2,1024,64]{1,2,0:T(8,128)}), f32[2,128,64]{1,2,0:T(8,128)}) %reduce-scatter.2.cloned.1.call-update) | async-done | bytes 65552 | tf_op jit(solution)/shard_map/reduce_scatter | solution.py:23
  189.4 0.0 all-reduce.5.cloned.1.call-update
  189.4 32.9 %all-reduce.5.cloned.1.call-done = f32[2,128,64]{1,2,0:T(8,128)} async-done(((f32[2,128,64]{1,2,0:T(8,128)}), f32[2,128,64]{1,2,0:T(8,128)}) %all-reduce.5.cloned.1.call-update) | async-done | bytes 65552 | tf_op jit(solution)/shard_map/psum | solution.py:24
  222.3 31.8 %all_gather.3 = f32[2,1024,64]{1,2,0:T(8,128)S(1)} all-gather(f32[2,128,64]{1,2,0:T(8,128)} %all-reduce.5.cloned.1.call-done), channel_id=1, replica_groups=mesh['rep'=4,'shard'=8] {'shard'}, dimensions={1}, use_global_device_ids=true | all-gather | bytes 589824 | tf_op jit(solution)/shard_map/all_gather | solution.py:25
  254.1 0.0 copy-start.1
  254.1 13.3 %fusion.4 = (f32[1,2,1024,1024]{3,2,1,0:T(8,128)}, bf16[2,1024,1024]{2,1,0:T(8,128)(2,1)}) fusion(f32[1,2,1024,1024]{3,2,1,0:T(8,128)} %param.4, bf16[1,2,1024,1024]{3,2,1,0:T(8,128)(2,1)} %param.3, f32[2,1024,64]{1,2,0:T(8,128)S(1)} %fusion.5, f32[2,1024,64]{1,2,0:T(8,128)S(1)} %broadcast_multiply_fusion), kind=kOutput, calls=%fused_computation.5 | convolution fusion | flops 1619001344 | bytes 26214400 | tf_op jit(solution)/shard_map/mrk,mck->mrc/dot_general | solution.py:26
  267.4 0.0 copy-done.1
  (5 shorter events, 0.1 us)
Async XLA Ops:
  7.2 1.0 copy-start
  7.2 49.8 %all-reduce.3.cloned.1.call-start = ((), (), s32[]{:S(2)}) async-start(), calls=%async_computation.1 | async-start | bytes 1048576 | tf_op jit(solution)/shard_map/psum | solution.py:18
  20.6 168.7 %reduce-scatter.2.cloned.1.call-start = ((), (), s32[]{:S(2)}) async-start(), calls=%async_computation.2 | async-start | bytes 589824 | tf_op jit(solution)/shard_map/reduce_scatter | solution.py:23
  129.6 92.7 %all-reduce.5.cloned.1.call-start = ((), (), s32[]{:S(2)}) async-start(), calls=%async_computation.3 | async-start | bytes 131072 | tf_op jit(solution)/shard_map/psum | solution.py:24
  254.1 13.3 %copy-start.1 = (f32[2,1024,64]{1,2,0:T(8,128)}, f32[2,1024,64]{1,2,0:T(8,128)S(1)}, u32[]{:S(2)}) copy-start(f32[2,1024,64]{1,2,0:T(8,128)S(1)} %broadcast_multiply_fusion) | copy-start | bytes 1572868
Sparse Core Ops, SparseCore 0:
  20.8 36.1 all-reduce.2
  129.7 59.6 reduce-scatter.1
  191.7 30.5 all-reduce.4
where the time goes:
time: 274 us
  waiting for transfers between devices  129 us (47%)
  blocking collectives  69.3 us (25%)
  matrix products  38.9 us (14%)
  other arithmetic  21.9 us (8%)
  between operations  13.8 us (5%)
    reduce_scatter x1, waiting for transfers between devices, on_device(): lax.psum_scatter(local_right, 'shard', scatter_dimension=1, tiled=True)  59.7 us
    psum x1, blocking collectives, on_device(): gram = lax.psum(local_gram, 'shard')  37.5 us
    psum x1, waiting for transfers between devices, on_device(): left = lax.psum(local_left, 'rep') / replicas  36.2 us
    psum x1, waiting for transfers between devices, on_device(): shares = lax.psum(shares, 'rep')  32.9 us
    all_gather x1, blocking collectives, on_device(): right = lax.all_gather(shares, 'shard', axis=1, tiled=True) / replicas  31.8 us
    dot_general x1, matrix products, on_device(): approx = jnp.einsum('mrk,mck->mrc', ortho, right, precision=highest)  13.3 us
    dot_general x1, matrix products, on_device(): local_left = jnp.einsum('mrc,mck->mrk', merged, basis_kv, precision=highest)  12.4 us
    another operation x4, other arithmetic, orthogonal(): chol = jnp.linalg.cholesky(gram)  11.9 us
  transfers between devices with their start and end apart: 3, of which 3 were waited for; matrix products, arithmetic and copies ran while one was open for 0% of the time, Pallas kernels for 0%

commit v1 on v0

v1 whole, which is shorter than its diff:
```python
import functools

import jax
import jax.numpy as jnp
from jax import lax
from jax.experimental import pallas as pl
from jax.experimental.pallas import tpu as pltpu
from jax.sharding import PartitionSpec as P

AXES = ("rep", "shard")
F32, BF16 = jnp.float32, jnp.bfloat16
HIGHEST = lax.Precision.HIGHEST
NT = (((1,), (1,)), ((), ()))
TN = (((0,), (0,)), ((), ()))
NN = (((1,), (0,)), ((), ()))


def dot(a, b, dims, precision=None):
    return lax.dot_general(a, b, dims, precision=precision, preferred_element_type=F32)


def split(x):
    high = x.astype(BF16)
    return high, (x - high.astype(F32)).astype(BF16)


def params(mib, axes=1):
    return pltpu.CompilerParams(
        vmem_limit_bytes=mib << 20, dimension_semantics=("arbitrary",) * axes
    )


def left_kernel(which, grad, error, basis, high, low, left, cut):
    rank = basis.shape[1]

    @pl.when(pl.program_id(0) == 0)
    def _():
        top, rest = split(basis[0])
        cut[:rank] = top
        cut[rank:] = rest

    merged = grad[0, 0].astype(F32) + error[0, 0]
    top, rest = split(merged)
    high[...] = top
    low[...] = rest
    both = dot(cut[...], top, NT)
    left[...] = both[:rank] + both[rank:] + dot(cut[:rank], rest, NT)


def left_of(which, grad, error, basis):
    _, _, rows, cols = grad.shape
    rank = basis.shape[1]
    block = min(rows, 256)
    tile = pl.BlockSpec((1, 1, block, cols), lambda i, w: (0, w[0], i, 0))
    flat = pl.BlockSpec((block, cols), lambda i, w: (i, 0))
    return pl.pallas_call(
        left_kernel,
        name="left",
        grid_spec=pltpu.PrefetchScalarGridSpec(
            num_scalar_prefetch=1,
            grid=(rows // block,),
            in_specs=[tile, tile, pl.BlockSpec((1, rank, cols), lambda i, w: (w[0], 0, 0))],
            out_specs=[flat, flat, pl.BlockSpec((rank, block), lambda i, w: (0, i))],
            scratch_shapes=[pltpu.VMEM((2 * rank, cols), BF16)],
        ),
        out_shape=[
            jax.ShapeDtypeStruct((rows, cols), BF16),
            jax.ShapeDtypeStruct((rows, cols), BF16),
            jax.ShapeDtypeStruct((rank, rows), F32),
        ],
        compiler_params=params(24),
        cost_estimate=pl.CostEstimate(
            flops=6 * rows * cols * rank, bytes_accessed=10 * rows * cols, transcendentals=0
        ),
    )(which, grad, error, basis)


def right_kernel(left, high, low, right):
    rank = left.shape[0]
    top, rest = split(left[...])
    both = dot(jnp.concatenate([top, rest], axis=0), high[...], NN)
    right[...] = both[:rank] + both[rank:] + dot(top, low[...], NN)


def right_of(left, high, low, part, parts):
    rows, cols = high.shape
    rank = left.shape[0]
    width = cols // parts
    block = min(width, 256)
    steps = width // block
    tile = pl.BlockSpec((rows, block), lambda i: (0, part * steps + i))
    return pl.pallas_call(
        right_kernel,
        name="right",
        grid=(steps,),
        in_specs=[pl.BlockSpec((rank, rows), lambda i: (0, 0)), tile, tile],
        out_specs=pl.BlockSpec((rank, block), lambda i: (0, i)),
        out_shape=jax.ShapeDtypeStruct((rank, width), F32),
        compiler_params=params(24),
        cost_estimate=pl.CostEstimate(
            flops=6 * rows * width * rank, bytes_accessed=4 * rows * width, transcendentals=0
        ),
    )(left, high, low)


def gram_kernel(scale, mine, theirs, left, gram):
    left[...] = (mine[...] + theirs[...]) * scale
    gram[...] = dot(left[...], left[...], NT, HIGHEST)


def gram_of(mine, theirs, scale):
    rank, rows = mine.shape
    return pl.pallas_call(
        functools.partial(gram_kernel, scale),
        name="gram",
        out_shape=[
            jax.ShapeDtypeStruct((rank, rows), F32),
            jax.ShapeDtypeStruct((rank, rank), F32),
        ],
        compiler_params=params(8, 0),
        cost_estimate=pl.CostEstimate(
            flops=12 * rank * rank * rows, bytes_accessed=12 * rank * rows, transcendentals=0
        ),
    )(mine, theirs)


def factor_kernel(gram, theirs, inverse):
    rank = gram.shape[0]
    row = lax.broadcasted_iota(jnp.int32, (rank, rank), 0)
    col = lax.broadcasted_iota(jnp.int32, (rank, rank), 1)
    eye = jnp.where(row == col, 1.0, 0.0)
    work = jnp.concatenate([gram[...] + theirs[...], eye], axis=1)
    below = lax.broadcasted_iota(jnp.int32, (rank, 1), 0)
    for j in range(rank - 1):
        pivot = work[j : j + 1, :]
        scaled = pivot * (1.0 / work[j : j + 1, j : j + 1])
        factor = jnp.where(below > j, work[:, j : j + 1], 0.0)
        work = work - factor * scaled
    diagonal = jnp.sum(work[:, :rank] * eye, axis=1, keepdims=True)
    inverse[...] = work[:, rank:] / jnp.sqrt(diagonal)


def factor_of(gram, theirs):
    rank = gram.shape[0]
    return pl.pallas_call(
        factor_kernel,
        name="factor",
        out_shape=jax.ShapeDtypeStruct((rank, rank), F32),
        compiler_params=params(8, 0),
        cost_estimate=pl.CostEstimate(
            flops=4 * rank**3, bytes_accessed=12 * rank * rank, transcendentals=rank
        ),
    )(gram, theirs)


def apply_kernel(scale, inverse, mine, theirs, out):
    out[...] = dot(inverse[...], (mine[...] + theirs[...]) * scale, NN, HIGHEST)


def apply_of(inverse, mine, theirs, scale):
    return pl.pallas_call(
        functools.partial(apply_kernel, scale),
        name="apply",
        out_shape=jax.ShapeDtypeStruct(mine.shape, F32),
        compiler_params=params(8, 0),
    )(inverse, mine, theirs)


def final_kernel(which, inverse, left, right, high, low, *refs):
    update, new_error, basis_next, ortho = refs[-4:]
    rank = left.shape[0]

    @pl.when(pl.program_id(0) == 0)
    def _():
        top, rest = split(dot(inverse[...], left[...], NN, HIGHEST))
        ortho[:rank] = top
        ortho[rank : 2 * rank] = top
        ortho[2 * rank :] = rest

    top, rest = split(right[...])
    approx = dot(ortho[...], jnp.concatenate([top, rest, top], axis=0), TN)
    update[0] = approx.astype(BF16)
    new_error[0, 0] = (high[...].astype(F32) + low[...].astype(F32)) - approx
    basis_next[0] = right[...]


def final_of(which, inverse, left, right, high, low, outs, part, parts):
    rows, cols = high.shape
    rank = left.shape[0]
    width = cols // parts
    block = min(width, 256)
    steps = width // block
    tile = pl.BlockSpec((rows, block), lambda i, w: (0, part * steps + i))
    whole = lambda shape: pl.BlockSpec(shape, lambda i, w: (0, 0))
    return pl.pallas_call(
        final_kernel,
        name="final",
        grid_spec=pltpu.PrefetchScalarGridSpec(
            num_scalar_prefetch=1,
            grid=(steps,),
            in_specs=[
                whole((rank, rank)),
                whole((rank, rows)),
                pl.BlockSpec((rank, block), lambda i, w: (0, i)),
                tile,
                tile,
            ]
            + [pl.BlockSpec(memory_space=pl.ANY)] * len(outs),
            out_specs=[
                pl.BlockSpec((1, rows, block), lambda i, w: (w[0], 0, part * steps + i)),
                pl.BlockSpec((1, 1, rows, block), lambda i, w: (0, w[0], 0, part * steps + i)),
                pl.BlockSpec((1, rank, block), lambda i, w: (w[0], 0, part * steps + i)),
            ],
            scratch_shapes=[pltpu.VMEM((3 * rank, rows), BF16)],
        ),
        out_shape=[
            jax.ShapeDtypeStruct((2, rows, cols), BF16),
            jax.ShapeDtypeStruct((1, 2, rows, cols), F32),
            jax.ShapeDtypeStruct((2, rank, cols), F32),
        ],
        input_output_aliases={6 + k: k for k in range(len(outs))},
        compiler_params=params(32),
        cost_estimate=pl.CostEstimate(
            flops=6 * rows * width * rank, bytes_accessed=10 * rows * width, transcendentals=0
        ),
    )(which, inverse, left, right, high, low, *outs)


def bits_of(count):
    return [1 << k for k in range(count.bit_length() - 1)]


def on_device(replicas, shards, grad_kv, error_kv, basis_kv):
    def swap(value, rep_mask, shard_mask):
        pairs = [
            (r * shards + s, (r ^ rep_mask) * shards + (s ^ shard_mask))
            for r in range(replicas)
            for s in range(shards)
        ]
        return lax.ppermute(value, AXES, pairs)

    core = functools.partial(swap, rep_mask=1, shard_mask=0)
    rep_steps = [(mask, 0) for mask in bits_of(replicas)[1:]]
    masks = bits_of(shards)
    masks[-1] |= masks[-2]
    shard_steps = [(0, mask) for mask in masks]
    scale = 1.0 / replicas

    basis = basis_kv.transpose(0, 2, 1)
    mine = (lax.axis_index("rep") % 2).astype(jnp.int32).reshape(1)
    theirs = 1 - mine

    high_t, low_t, left_t = left_of(theirs, grad_kv, error_kv, basis)
    arriving = core(left_t)
    high_m, low_m, left_m = left_of(mine, grad_kv, error_kv, basis)
    left_m = left_m + arriving
    for step in rep_steps[:-1]:
        left_m = left_m + swap(left_m, *step)
    left_m, gram = gram_of(left_m, swap(left_m, *rep_steps[-1]), scale)
    left_t = core(left_m)

    for step in shard_steps[:-1]:
        gram = gram + swap(gram, *step)
    inverse_m = factor_of(gram, swap(gram, *shard_steps[-1]))
    inverse_t = core(inverse_m)

    orders = (rep_steps + shard_steps, shard_steps[:1] + rep_steps + shard_steps[:0:-1])
    parts = len(orders)
    rights = []
    for part, order in enumerate(orders):
        right_t = core(right_of(left_t, high_t, low_t, part, parts))
        right = right_of(left_m, high_m, low_m, part, parts) + right_t
        for step in order[:-1]:
            right = right + swap(right, *step)
        right_m = apply_of(inverse_m, right, swap(right, *order[-1]), scale)
        rights.append((right_m, core(right_m)))

    outs = ()
    for part, (right_m, right_t) in enumerate(rights):
        outs = final_of(mine, inverse_m, left_m, right_m, high_m, low_m, outs, part, parts)
        outs = final_of(theirs, inverse_t, left_t, right_t, high_t, low_t, outs, part, parts)
    update, new_error, right = outs
    return update, new_error, right.transpose(0, 2, 1)


def solution(mesh):
    placed = (P("rep", None, "shard", None), P("rep", None, "shard", None), P())
    return jax.shard_map(
        functools.partial(on_device, mesh.shape["rep"], mesh.shape["shard"]),
        mesh=mesh,
        in_specs=placed,
        out_specs=(P(None, "shard", None), P("rep", None, "shard", None), P()),
        check_vma=False,
    )
```

time: 274 us -> 84.7 us (0.31)
  waiting for transfers between devices: 129 us -> 23.5 us
  blocking collectives: 69.3 us -> 0 us
  matrix products: 38.9 us -> 0 us
  starting transfers between devices: 0.12 us -> 26.1 us
  Pallas kernels: 0 us -> 25.1 us
  other arithmetic: 21.9 us -> 0.2 us
  between operations: 13.8 us -> 0.84 us
  local copies, waits for them, and re-layouts: 1.08 us -> 8.64 us
    psum x2 -> x0, waiting for transfers between devices: 69.1 us -> none  [the longest x1 36.2 us: on_device(): left = lax.psum(local_left, 'rep') / replicas]
    reduce_scatter x1 -> x0, waiting for transfers between devices: 59.7 us -> none  [on_device(): lax.psum_scatter(local_right, 'shard', scatter_dimension=1, tiled=True)]
    psum x1 -> x0, blocking collectives: 37.5 us -> none  [on_device(): gram = lax.psum(local_gram, 'shard')]
    dot_general x4 -> x0, matrix products: 37.2 us -> none  [the longest x1 13.3 us: on_device(): approx = jnp.einsum('mrk,mck->mrc', ortho, right, precision=highest)]
    all_gather x1 -> x0, blocking collectives: 31.8 us -> none  [on_device(): right = lax.all_gather(shares, 'shard', axis=1, tiled=True) / replicas]
    ppermute x0 -> x19, starting transfers between devices: none -> 26.1 us  [swap(): return lax.ppermute(value, AXES, pairs)]
    pallas_call x0 -> x14, Pallas kernels: none -> 25.1 us  [the longest x4 11.1 us: final_of(): pl.pallas_call(final_kernel, name='final', grid_spec=pltpu.PrefetchScalar...]
    ppermute x0 -> x19, waiting for transfers between devices: none -> 23.5 us  [swap(): return lax.ppermute(value, AXES, pairs)]
  transfers between devices with their start and end apart: 3 -> 19, of which waited for: 3 -> 10; matrix products, arithmetic and copies ran while one was open for 0% -> 0% of each run, Pallas kernels for 0% -> 23%
where the time goes in v1:
time: 84.7 us; the launch traced here: 84.4 us
  starting transfers between devices  26.1 us (31%)
  Pallas kernels  25.1 us (30%)
  waiting for transfers between devices  23.5 us (28%)
  local copies, waits for them, and re-layouts  8.64 us (10%)
    ppermute x19, starting transfers between devices, swap(): return lax.ppermute(value, AXES, pairs)  26.1 us
    ppermute x19, waiting for transfers between devices, swap(): return lax.ppermute(value, AXES, pairs)  23.5 us
    pallas_call x4, Pallas kernels, final_of(): pl.pallas_call(final_kernel, name='final', grid_spec=pltpu.PrefetchScalar...  11.1 us
    unnamed x10, local copies, waits for them, and re-layouts  8.64 us
    pallas_call x1, Pallas kernels, factor_of(): pl.pallas_call(factor_kernel, name='factor', out_shape=jax.ShapeDtypeStru...  5.46 us
    pallas_call x2, Pallas kernels, left_of(): pl.pallas_call(left_kernel, name='left', grid_spec=pltpu.PrefetchScalarGr...  3.94 us
    pallas_call x4, Pallas kernels, right_of(): pl.pallas_call(right_kernel, name='right', grid=(steps,), in_specs=[pl.Bl...  3.75 us
  transfers between devices with their start and end apart: 19, of which 10 were waited for; matrix products, arithmetic and copies ran while one was open for 0% of the time, Pallas kernels for 23%

profile of v1, /device:TPU:0, one launch (start us, length us, event | category | flops | bytes accessed | tf_op | source)
XLA Modules:
  0.0 84.4 jit_solution(14025233501801146159)
XLA Ops:
  0.7 3.4 %copy-done = f32[1,2,1024,1024]{3,2,1,0:T(8,128)S(1)} copy-done((f32[1,2,1024,1024]{3,2,1,0:T(8,128)S(1)}, f32[1,2,1024,1024]{3,2,1,0:T(8,128)}, u32[]{:S(2)}) %copy-start) | copy-done | bytes 8388632
  4.0 2.2 %copy-done.2 = bf16[1,2,1024,1024]{3,2,1,0:T(8,128)(2,1)S(1)} copy-done((bf16[1,2,1024,1024]{3,2,1,0:T(8,128)(2,1)S(1)}, bf16[1,2,1024,1024]{3,2,1,0:T(8,128)(2,1)}, u32[]{:S(2)}) %copy-start.2) | copy-done | bytes 4194328
  6.2 1.0 %copy-done.4 = f32[2,1024,64]{1,2,0:T(8,128)S(1)} copy-done((f32[2,1024,64]{1,2,0:T(8,128)S(1)}, f32[2,1024,64]{1,2,0:T(8,128)}, u32[]{:S(2)}) %copy-start.4) | copy-done | bytes 524312
  7.3 2.0 %left.3 = (bf16[1024,1024]{1,0:T(8,128)(2,1)S(1)}, bf16[1024,1024]{1,0:T(8,128)(2,1)S(1)}, f32[64,1024]{1,0:T(8,128)S(1)}) custom-call(s32[1]{0:T(128)S(6)} %sub.3.which, bf16[1,2,1024,1024]{3,2,1,0:T(8,128)(2,1)S(1)} %copy-done.2, f32[1,2,1024,1024]{3,2,1,0:T(8,128)S(1)} %copy-done, f32[2,64,1024]{2,1,0:T(8,128)S(1)} %bitcast.3), custom_call_target="tpu_custom_call" | custom-call | flops 402653184 | bytes 10485760 | tf_op jit(solution)/shard_map/left/pallas_call | solution.py:56
  9.2 0.6 collective-permute-start
  9.8 0.8 %copy-done.1 = f32[1,2,1024,1024]{3,2,1,0:T(8,128)S(1)} copy-done((f32[1,2,1024,1024]{3,2,1,0:T(8,128)S(1)}, f32[1,2,1024,1024]{3,2,1,0:T(8,128)}, u32[]{:S(2)}) %copy-start.1) | copy-done | bytes 8388632
  10.6 1.2 %copy-done.3 = bf16[1,2,1024,1024]{3,2,1,0:T(8,128)(2,1)S(1)} copy-done((bf16[1,2,1024,1024]{3,2,1,0:T(8,128)(2,1)S(1)}, bf16[1,2,1024,1024]{3,2,1,0:T(8,128)(2,1)}, u32[]{:S(2)}) %copy-start.3) | copy-done | bytes 4194328
  11.8 2.0 %left.2 = (bf16[1024,1024]{1,0:T(8,128)(2,1)S(1)}, bf16[1024,1024]{1,0:T(8,128)(2,1)S(1)}, f32[64,1024]{1,0:T(8,128)S(1)}) custom-call(s32[1]{0:T(128)} %bitcast.which, bf16[1,2,1024,1024]{3,2,1,0:T(8,128)(2,1)S(1)} %copy-done.3, f32[1,2,1024,1024]{3,2,1,0:T(8,128)S(1)} %copy-done.1, f32[2,64,1024]{2,1,0:T(8,128)S(1)} %bitcast.4), custom_call_target="tpu_custom_call" | custom-call | flops 402653184 | bytes 10485760 | tf_op jit(solution)/shard_map/left/pallas_call | solution.py:56
  13.9 3.1 %collective-permute-start.1 = (f32[64,1024]{1,0:T(8,128)S(1)}, f32[64,1024]{1,0:T(8,128)S(1)}, u32[]{:S(2)}, u32[]{:S(2)}) collective-permute-start(f32[64,1024]{1,0:T(8,128)S(1)} %add.38.mine), channel_id=1, source_target_pairs={{0,16},{1,17},{2,18},{3,19},{4,20},{5,21},{6,22},{7,23},{8,24},{9,... | collective-permute-start | bytes 786440 | tf_op jit(solution)/shard_map/ppermute | solution.py:240
  16.9 6.3 %collective-permute-done.1.theirs = f32[64,1024]{1,0:T(8,128)S(1)} collective-permute-done((f32[64,1024]{1,0:T(8,128)S(1)}, f32[64,1024]{1,0:T(8,128)S(1)}, u32[]{:S(2)}, u32[]{:S(2)}) %collective-permute-start.1) | collective-permute-done | bytes 262176 | tf_op jit(solution)/shard_map/ppermute | solution.py:240
  23.2 0.4 gram.1
  23.6 0.1 collective-permute-start.6
  23.7 1.5 %collective-permute-done.6.left = f32[64,1024]{1,0:T(8,128)S(1)} collective-permute-done((f32[64,1024]{1,0:T(8,128)S(1)}, f32[64,1024]{1,0:T(8,128)S(1)}, u32[]{:S(2)}, u32[]{:S(2)}) %collective-permute-start.6) | collective-permute-done | bytes 262176 | tf_op jit(solution)/shard_map/ppermute | solution.py:240
  25.2 0.9 %right.7 = f32[64,512]{1,0:T(8,128)S(1)} custom-call(f32[64,1024]{1,0:T(8,128)S(1)} %collective-permute-done.6.left, bf16[1024,1024]{1,0:T(8,128)(2,1)S(1)} %get-tuple-element.29.high, bf16[1024,1024]{1,0:T(8,128)(2,1)S(1)} %get-tuple-element.30.low), custom_call_target="tpu_custom_call" | custom-call | flops 201326592 | bytes 2097152 | tf_op jit(solution)/shard_map/right/pallas_call | solution.py:92
  26.2 0.2 collective-permute-start.13
  26.4 0.9 %right.5 = f32[64,512]{1,0:T(8,128)S(1)} custom-call(f32[64,1024]{1,0:T(8,128)S(1)} %collective-permute-done.6.left, bf16[1024,1024]{1,0:T(8,128)(2,1)S(1)} %get-tuple-element.29.high, bf16[1024,1024]{1,0:T(8,128)(2,1)S(1)} %get-tuple-element.30.low), custom_call_target="tpu_custom_call" | custom-call | flops 201326592 | bytes 2097152 | tf_op jit(solution)/shard_map/right/pallas_call | solution.py:92
  27.3 0.4 collective-permute-start.7
  27.7 0.9 %right.6 = f32[64,512]{1,0:T(8,128)S(1)} custom-call(f32[64,1024]{1,0:T(8,128)S(1)} %get-tuple-element.26.left, bf16[1024,1024]{1,0:T(8,128)(2,1)S(1)} %get-tuple-element.27.high, bf16[1024,1024]{1,0:T(8,128)(2,1)S(1)} %get-tuple-element.28.low), custom_call_target="tpu_custom_call" | custom-call | flops 201326592 | bytes 2097152 | tf_op jit(solution)/shard_map/right/pallas_call | solution.py:92
  28.7 1.8 %collective-permute-start.14 = (f32[64,512]{1,0:T(8,128)S(1)}, f32[64,512]{1,0:T(8,128)S(1)}, u32[]{:S(2)}, u32[]{:S(2)}) collective-permute-start(f32[64,512]{1,0:T(8,128)S(1)} %add.45), channel_id=1, source_target_pairs={{0,16},{1,17},{2,18},{3,19},{4,20},{5,21},{6,22},{7,23},{8,24},{9,... | collective-permute-start | bytes 393224 | tf_op jit(solution)/shard_map/ppermute | solution.py:240
  30.5 0.9 %right.4 = f32[64,512]{1,0:T(8,128)S(1)} custom-call(f32[64,1024]{1,0:T(8,128)S(1)} %get-tuple-element.26.left, bf16[1024,1024]{1,0:T(8,128)(2,1)S(1)} %get-tuple-element.27.high, bf16[1024,1024]{1,0:T(8,128)(2,1)S(1)} %get-tuple-element.28.low), custom_call_target="tpu_custom_call" | custom-call | flops 201326592 | bytes 2097152 | tf_op jit(solution)/shard_map/right/pallas_call | solution.py:92
  31.5 1.6 %collective-permute-start.8 = (f32[64,512]{1,0:T(8,128)S(1)}, f32[64,512]{1,0:T(8,128)S(1)}, u32[]{:S(2)}, u32[]{:S(2)}) collective-permute-start(f32[64,512]{1,0:T(8,128)S(1)} %add.41), channel_id=1, source_target_pairs={{0,1},{1,0},{2,3},{3,2},{4,5},{5,4},{6,7},{7,6},{8,9},{9,8},{10,11... | collective-permute-start | bytes 393224 | tf_op jit(solution)/shard_map/ppermute | solution.py:240
  33.1 1.3 %collective-permute-done.14 = f32[64,512]{1,0:T(8,128)S(1)} collective-permute-done((f32[64,512]{1,0:T(8,128)S(1)}, f32[64,512]{1,0:T(8,128)S(1)}, u32[]{:S(2)}, u32[]{:S(2)}) %collective-permute-start.14) | collective-permute-done | bytes 131104 | tf_op jit(solution)/shard_map/ppermute | solution.py:240
  34.4 1.8 %collective-permute-start.15 = (f32[64,512]{1,0:T(8,128)S(1)}, f32[64,512]{1,0:T(8,128)S(1)}, u32[]{:S(2)}, u32[]{:S(2)}) collective-permute-start(f32[64,512]{1,0:T(8,128)S(1)} %add.46), channel_id=1, source_target_pairs={{0,1},{1,0},{2,3},{3,2},{4,5},{5,4},{6,7},{7,6},{8,9},{9,8},{10,11... | collective-permute-start | bytes 393224 | tf_op jit(solution)/shard_map/ppermute | solution.py:240
  36.1 1.3 %collective-permute-done.8 = f32[64,512]{1,0:T(8,128)S(1)} collective-permute-done((f32[64,512]{1,0:T(8,128)S(1)}, f32[64,512]{1,0:T(8,128)S(1)}, u32[]{:S(2)}, u32[]{:S(2)}) %collective-permute-start.8) | collective-permute-done | bytes 131104 | tf_op jit(solution)/shard_map/ppermute | solution.py:240
  37.4 0.3 collective-permute-start.9
  37.7 1.9 %collective-permute-done.15 = f32[64,512]{1,0:T(8,128)S(1)} collective-permute-done((f32[64,512]{1,0:T(8,128)S(1)}, f32[64,512]{1,0:T(8,128)S(1)}, u32[]{:S(2)}, u32[]{:S(2)}) %collective-permute-start.15) | collective-permute-done | bytes 131104 | tf_op jit(solution)/shard_map/ppermute | solution.py:240
  39.7 1.6 %collective-permute-start.16 = (f32[64,512]{1,0:T(8,128)S(1)}, f32[64,512]{1,0:T(8,128)S(1)}, u32[]{:S(2)}, u32[]{:S(2)}) collective-permute-start(f32[64,512]{1,0:T(8,128)S(1)} %add.47), channel_id=1, source_target_pairs={{0,2},{1,3},{2,0},{3,1},{4,6},{5,7},{6,4},{7,5},{8,10},{9,11},{10,... | collective-permute-start | bytes 393224 | tf_op jit(solution)/shard_map/ppermute | solution.py:240
  41.3 1.1 %collective-permute-done.9 = f32[64,512]{1,0:T(8,128)S(1)} collective-permute-done((f32[64,512]{1,0:T(8,128)S(1)}, f32[64,512]{1,0:T(8,128)S(1)}, u32[]{:S(2)}, u32[]{:S(2)}) %collective-permute-start.9) | collective-permute-done | bytes 131104 | tf_op jit(solution)/shard_map/ppermute | solution.py:240
  42.5 3.5 %collective-permute-start.10 = (f32[64,512]{1,0:T(8,128)S(1)}, f32[64,512]{1,0:T(8,128)S(1)}, u32[]{:S(2)}, u32[]{:S(2)}) collective-permute-start(f32[64,512]{1,0:T(8,128)S(1)} %add.43), channel_id=1, source_target_pairs={{0,6},{1,7},{2,4},{3,5},{4,2},{5,3},{6,0},{7,1},{8,14},{9,15},{10,... | collective-permute-start | bytes 393224 | tf_op jit(solution)/shard_map/ppermute | solution.py:240
  46.0 3.9 %collective-permute-start.17 = (f32[64,512]{1,0:T(8,128)S(1)}, f32[64,512]{1,0:T(8,128)S(1)}, u32[]{:S(2)}, u32[]{:S(2)}) collective-permute-start(f32[64,512]{1,0:T(8,128)S(1)} %add.48.mine), channel_id=1, source_target_pairs={{0,6},{1,7},{2,4},{3,5},{4,2},{5,3},{6,0},{7,1},{8,14},{9,15},{10,... | collective-permute-start | bytes 393224 | tf_op jit(solution)/shard_map/ppermute | solution.py:240
  49.8 0.9 %collective-permute-done.10 = f32[64,512]{1,0:T(8,128)S(1)} collective-permute-done((f32[64,512]{1,0:T(8,128)S(1)}, f32[64,512]{1,0:T(8,128)S(1)}, u32[]{:S(2)}, u32[]{:S(2)}) %collective-permute-start.10) | collective-permute-done | bytes 131104 | tf_op jit(solution)/shard_map/ppermute | solution.py:240
  50.7 2.3 %collective-permute-start.11 = (f32[64,512]{1,0:T(8,128)S(1)}, f32[64,512]{1,0:T(8,128)S(1)}, u32[]{:S(2)}, u32[]{:S(2)}) collective-permute-start(f32[64,512]{1,0:T(8,128)S(1)} %add.44.mine), channel_id=1, source_target_pairs={{0,2},{1,3},{2,0},{3,1},{4,6},{5,7},{6,4},{7,5},{8,10},{9,11},{10,... | collective-permute-start | bytes 393224 | tf_op jit(solution)/shard_map/ppermute | solution.py:240
  53.1 1.5 %collective-permute-start.2 = (f32[64,64]{1,0:T(8,128)S(1)}, f32[64,64]{1,0:T(8,128)S(1)}, u32[]{:S(2)}, u32[]{:S(2)}) collective-permute-start(f32[64,64]{1,0:T(8,128)S(1)} %get-tuple-element.25), channel_id=1, source_target_pairs={{0,1},{1,0},{2,3},{3,2},{4,5},{5,4},{6,7},{7,6},{8,9},{9,8},{10,11... | collective-permute-start | bytes 49160 | tf_op jit(solution)/shard_map/ppermute | solution.py:240
  54.6 2.4 %collective-permute-done.2 = f32[64,64]{1,0:T(8,128)S(1)} collective-permute-done((f32[64,64]{1,0:T(8,128)S(1)}, f32[64,64]{1,0:T(8,128)S(1)}, u32[]{:S(2)}, u32[]{:S(2)}) %collective-permute-start.2) | collective-permute-done | bytes 16416 | tf_op jit(solution)/shard_map/ppermute | solution.py:240
  57.0 0.1 collective-permute-start.3
  57.1 3.8 %collective-permute-done.3 = f32[64,64]{1,0:T(8,128)S(1)} collective-permute-done((f32[64,64]{1,0:T(8,128)S(1)}, f32[64,64]{1,0:T(8,128)S(1)}, u32[]{:S(2)}, u32[]{:S(2)}) %collective-permute-start.3) | collective-permute-done | bytes 16416 | tf_op jit(solution)/shard_map/ppermute | solution.py:240
  60.9 2.7 %collective-permute-start.4 = (f32[64,64]{1,0:T(8,128)S(1)}, f32[64,64]{1,0:T(8,128)S(1)}, u32[]{:S(2)}, u32[]{:S(2)}) collective-permute-start(f32[64,64]{1,0:T(8,128)S(1)} %add.40.gram), channel_id=1, source_target_pairs={{0,6},{1,7},{2,4},{3,5},{4,2},{5,3},{6,0},{7,1},{8,14},{9,15},{10,... | collective-permute-start | bytes 49160 | tf_op jit(solution)/shard_map/ppermute | solution.py:240
  63.6 3.0 %collective-permute-done.4.theirs = f32[64,64]{1,0:T(8,128)S(1)} collective-permute-done((f32[64,64]{1,0:T(8,128)S(1)}, f32[64,64]{1,0:T(8,128)S(1)}, u32[]{:S(2)}, u32[]{:S(2)}) %collective-permute-start.4) | collective-permute-done | bytes 16416 | tf_op jit(solution)/shard_map/ppermute | solution.py:240
  66.6 5.5 %factor.1.inverse = f32[64,64]{1,0:T(8,128)S(1)} custom-call(f32[64,64]{1,0:T(8,128)S(1)} %add.40.gram, f32[64,64]{1,0:T(8,128)S(1)} %collective-permute-done.4.theirs), custom_call_target="tpu_custom_call" | custom-call | flops 1048576 | bytes 49152 | tf_op jit(solution)/shard_map/factor/pallas_call | solution.py:145
  72.1 0.3 apply.3.right
  72.4 0.1 collective-permute-start.18
  72.4 0.3 apply.2.right
  72.7 0.5 collective-permute-start.12
  73.3 0.1 collective-permute-start.5
  73.4 2.8 %final.4 = (bf16[2,1024,1024]{2,1,0:T(8,128)(2,1)}, f32[1,2,1024,1024]{3,2,1,0:T(8,128)}, f32[2,64,1024]{2,1,0:T(8,128)}) custom-call(s32[1]{0:T(128)} %bitcast.which, f32[64,64]{1,0:T(8,128)S(1)} %factor.1.inverse, f32[64,1024]{1,0:T(8,128)S(1)} %get-tuple-element.26.left, f32[64,512]{1,0:T(8,128)S(1)} %apply.3.right, ...), custom_call_target="tpu_custom_call" | custom-call | flops 201326592 | bytes 5242880 | tf_op jit(solution)/shard_map/final/pallas_call | solution.py:195
  76.1 2.8 %final.5 = (bf16[2,1024,1024]{2,1,0:T(8,128)(2,1)}, f32[1,2,1024,1024]{3,2,1,0:T(8,128)}, f32[2,64,1024]{2,1,0:T(8,128)}) custom-call(s32[1]{0:T(128)S(6)} %sub.3.which, f32[64,64]{1,0:T(8,128)S(1)} %collective-permute-done.5.inverse, f32[64,1024]{1,0:T(8,128)S(1)} %collective-permute-done.6.left, ...), custom_call_target="tpu_custom_call", output_to_operand_aliasing={{0}: (6, {}), {1}: (7, {}), {2}: (8, {})} | custom-call | flops 201326592 | bytes 5242880 | tf_op jit(solution)/shard_map/final/pallas_call | solution.py:195
  78.9 2.8 %final.6 = (bf16[2,1024,1024]{2,1,0:T(8,128)(2,1)}, f32[1,2,1024,1024]{3,2,1,0:T(8,128)}, f32[2,64,1024]{2,1,0:T(8,128)}) custom-call(s32[1]{0:T(128)} %bitcast.which, f32[64,64]{1,0:T(8,128)S(1)} %factor.1.inverse, f32[64,1024]{1,0:T(8,128)S(1)} %get-tuple-element.26.left, ...), custom_call_target="tpu_custom_call", output_to_operand_aliasing={{0}: (6, {}), {1}: (7, {}), {2}: (8, {})} | custom-call | flops 201326592 | bytes 5242880 | tf_op jit(solution)/shard_map/final/pallas_call | solution.py:195
  81.6 2.8 %final.7 = (bf16[2,1024,1024]{2,1,0:T(8,128)(2,1)}, f32[1,2,1024,1024]{3,2,1,0:T(8,128)}, f32[2,64,1024]{2,1,0:T(8,128)}) custom-call(s32[1]{0:T(128)S(6)} %sub.3.which, f32[64,64]{1,0:T(8,128)S(1)} %collective-permute-done.5.inverse, f32[64,1024]{1,0:T(8,128)S(1)} %collective-permute-done.6.left, ...), custom_call_target="tpu_custom_call", output_to_operand_aliasing={{0}: (6, {}), {1}: (7, {}), {2}: (8, {})} | custom-call | flops 201326592 | bytes 5242880 | tf_op jit(solution)/shard_map/final/pallas_call | solution.py:195
  (25 shorter events, 0.2 us)
Async XLA Ops:
  0.6 3.4 %copy-start = (f32[1,2,1024,1024]{3,2,1,0:T(8,128)S(1)}, f32[1,2,1024,1024]{3,2,1,0:T(8,128)}, u32[]{:S(2)}) copy-start(f32[1,2,1024,1024]{3,2,1,0:T(8,128)} %error.3) | copy-start | bytes 25165828
  4.0 2.2 %copy-start.2 = (bf16[1,2,1024,1024]{3,2,1,0:T(8,128)(2,1)S(1)}, bf16[1,2,1024,1024]{3,2,1,0:T(8,128)(2,1)}, u32[]{:S(2)}) copy-start(bf16[1,2,1024,1024]{3,2,1,0:T(8,128)(2,1)} %grad.3) | copy-start | bytes 12582916
  6.2 1.0 %copy-start.4 = (f32[2,1024,64]{1,2,0:T(8,128)S(1)}, f32[2,1024,64]{1,2,0:T(8,128)}, u32[]{:S(2)}) copy-start(f32[2,1024,64]{1,2,0:T(8,128)} %param.5) | copy-start | bytes 1572868
  7.3 3.4 %copy-start.1 = (f32[1,2,1024,1024]{3,2,1,0:T(8,128)S(1)}, f32[1,2,1024,1024]{3,2,1,0:T(8,128)}, u32[]{:S(2)}) copy-start(f32[1,2,1024,1024]{3,2,1,0:T(8,128)} %error.3) | copy-start | bytes 25165828
  7.3 4.6 %copy-start.3 = (bf16[1,2,1024,1024]{3,2,1,0:T(8,128)(2,1)S(1)}, bf16[1,2,1024,1024]{3,2,1,0:T(8,128)(2,1)}, u32[]{:S(2)}) copy-start(bf16[1,2,1024,1024]{3,2,1,0:T(8,128)(2,1)} %grad.3) | copy-start | bytes 12582916
  9.2 4.6 %collective-permute-start = (f32[64,1024]{1,0:T(8,128)S(1)}, f32[64,1024]{1,0:T(8,128)S(1)}, u32[]{:S(2)}, u32[]{:S(2)}) collective-permute-start(f32[64,1024]{1,0:T(8,128)S(1)} %get-tuple-element.24), channel_id=1, source_target_pairs={{0,8},{1,9},{2,10},{3,11},{4,12},{5,13},{6,14},{7,15},{8,0},{9,1},... | collective-permute-start | bytes 786440 | tf_op jit(solution)/shard_map/ppermute | solution.py:240
  13.9 9.4 %collective-permute-start.1 = (f32[64,1024]{1,0:T(8,128)S(1)}, f32[64,1024]{1,0:T(8,128)S(1)}, u32[]{:S(2)}, u32[]{:S(2)}) collective-permute-start(f32[64,1024]{1,0:T(8,128)S(1)} %add.38.mine), channel_id=1, source_target_pairs={{0,16},{1,17},{2,18},{3,19},{4,20},{5,21},{6,22},{7,23},{8,24},{9,... | collective-permute-start | bytes 786440 | tf_op jit(solution)/shard_map/ppermute | solution.py:240
  23.6 1.6 %collective-permute-start.6 = (f32[64,1024]{1,0:T(8,128)S(1)}, f32[64,1024]{1,0:T(8,128)S(1)}, u32[]{:S(2)}, u32[]{:S(2)}) collective-permute-start(f32[64,1024]{1,0:T(8,128)S(1)} %get-tuple-element.26.left), channel_id=1, source_target_pairs={{0,8},{1,9},{2,10},{3,11},{4,12},{5,13},{6,14},{7,15},{8,0},{9,1},... | collective-permute-start | bytes 786440 | tf_op jit(solution)/shard_map/ppermute | solution.py:240
  26.2 2.5 %collective-permute-start.13 = (f32[64,512]{1,0:T(8,128)S(1)}, f32[64,512]{1,0:T(8,128)S(1)}, u32[]{:S(2)}, u32[]{:S(2)}) collective-permute-start(f32[64,512]{1,0:T(8,128)S(1)} %right.7), channel_id=1, source_target_pairs={{0,8},{1,9},{2,10},{3,11},{4,12},{5,13},{6,14},{7,15},{8,0},{9,1},... | collective-permute-start | bytes 393224 | tf_op jit(solution)/shard_map/ppermute | solution.py:240
  27.3 4.2 %collective-permute-start.7 = (f32[64,512]{1,0:T(8,128)S(1)}, f32[64,512]{1,0:T(8,128)S(1)}, u32[]{:S(2)}, u32[]{:S(2)}) collective-permute-start(f32[64,512]{1,0:T(8,128)S(1)} %right.5), channel_id=1, source_target_pairs={{0,8},{1,9},{2,10},{3,11},{4,12},{5,13},{6,14},{7,15},{8,0},{9,1},... | collective-permute-start | bytes 393224 | tf_op jit(solution)/shard_map/ppermute | solution.py:240
  28.7 5.6 %collective-permute-start.14 = (f32[64,512]{1,0:T(8,128)S(1)}, f32[64,512]{1,0:T(8,128)S(1)}, u32[]{:S(2)}, u32[]{:S(2)}) collective-permute-start(f32[64,512]{1,0:T(8,128)S(1)} %add.45), channel_id=1, source_target_pairs={{0,16},{1,17},{2,18},{3,19},{4,20},{5,21},{6,22},{7,23},{8,24},{9,... | collective-permute-start | bytes 393224 | tf_op jit(solution)/shard_map/ppermute | solution.py:240
  31.5 5.9 %collective-permute-start.8 = (f32[64,512]{1,0:T(8,128)S(1)}, f32[64,512]{1,0:T(8,128)S(1)}, u32[]{:S(2)}, u32[]{:S(2)}) collective-permute-start(f32[64,512]{1,0:T(8,128)S(1)} %add.41), channel_id=1, source_target_pairs={{0,1},{1,0},{2,3},{3,2},{4,5},{5,4},{6,7},{7,6},{8,9},{9,8},{10,11... | collective-permute-start | bytes 393224 | tf_op jit(solution)/shard_map/ppermute | solution.py:240
  34.4 5.3 %collective-permute-start.15 = (f32[64,512]{1,0:T(8,128)S(1)}, f32[64,512]{1,0:T(8,128)S(1)}, u32[]{:S(2)}, u32[]{:S(2)}) collective-permute-start(f32[64,512]{1,0:T(8,128)S(1)} %add.46), channel_id=1, source_target_pairs={{0,1},{1,0},{2,3},{3,2},{4,5},{5,4},{6,7},{7,6},{8,9},{9,8},{10,11... | collective-permute-start | bytes 393224 | tf_op jit(solution)/shard_map/ppermute | solution.py:240
  37.4 5.0 %collective-permute-start.9 = (f32[64,512]{1,0:T(8,128)S(1)}, f32[64,512]{1,0:T(8,128)S(1)}, u32[]{:S(2)}, u32[]{:S(2)}) collective-permute-start(f32[64,512]{1,0:T(8,128)S(1)} %add.42), channel_id=1, source_target_pairs={{0,16},{1,17},{2,18},{3,19},{4,20},{5,21},{6,22},{7,23},{8,24},{9,... | collective-permute-start | bytes 393224 | tf_op jit(solution)/shard_map/ppermute | solution.py:240
  39.7 6.2 %collective-permute-start.16 = (f32[64,512]{1,0:T(8,128)S(1)}, f32[64,512]{1,0:T(8,128)S(1)}, u32[]{:S(2)}, u32[]{:S(2)}) collective-permute-start(f32[64,512]{1,0:T(8,128)S(1)} %add.47), channel_id=1, source_target_pairs={{0,2},{1,3},{2,0},{3,1},{4,6},{5,7},{6,4},{7,5},{8,10},{9,11},{10,... | collective-permute-start | bytes 393224 | tf_op jit(solution)/shard_map/ppermute | solution.py:240
  42.5 8.2 %collective-permute-start.10 = (f32[64,512]{1,0:T(8,128)S(1)}, f32[64,512]{1,0:T(8,128)S(1)}, u32[]{:S(2)}, u32[]{:S(2)}) collective-permute-start(f32[64,512]{1,0:T(8,128)S(1)} %add.43), channel_id=1, source_target_pairs={{0,6},{1,7},{2,4},{3,5},{4,2},{5,3},{6,0},{7,1},{8,14},{9,15},{10,... | collective-permute-start | bytes 393224 | tf_op jit(solution)/shard_map/ppermute | solution.py:240
  46.0 26.1 %collective-permute-start.17 = (f32[64,512]{1,0:T(8,128)S(1)}, f32[64,512]{1,0:T(8,128)S(1)}, u32[]{:S(2)}, u32[]{:S(2)}) collective-permute-start(f32[64,512]{1,0:T(8,128)S(1)} %add.48.mine), channel_id=1, source_target_pairs={{0,6},{1,7},{2,4},{3,5},{4,2},{5,3},{6,0},{7,1},{8,14},{9,15},{10,... | collective-permute-start | bytes 393224 | tf_op jit(solution)/shard_map/ppermute | solution.py:240
  50.7 21.7 %collective-permute-start.11 = (f32[64,512]{1,0:T(8,128)S(1)}, f32[64,512]{1,0:T(8,128)S(1)}, u32[]{:S(2)}, u32[]{:S(2)}) collective-permute-start(f32[64,512]{1,0:T(8,128)S(1)} %add.44.mine), channel_id=1, source_target_pairs={{0,2},{1,3},{2,0},{3,1},{4,6},{5,7},{6,4},{7,5},{8,10},{9,11},{10,... | collective-permute-start | bytes 393224 | tf_op jit(solution)/shard_map/ppermute | solution.py:240
  53.1 3.9 %collective-permute-start.2 = (f32[64,64]{1,0:T(8,128)S(1)}, f32[64,64]{1,0:T(8,128)S(1)}, u32[]{:S(2)}, u32[]{:S(2)}) collective-permute-start(f32[64,64]{1,0:T(8,128)S(1)} %get-tuple-element.25), channel_id=1, source_target_pairs={{0,1},{1,0},{2,3},{3,2},{4,5},{5,4},{6,7},{7,6},{8,9},{9,8},{10,11... | collective-permute-start | bytes 49160 | tf_op jit(solution)/shard_map/ppermute | solution.py:240
  57.0 3.9 %collective-permute-start.3 = (f32[64,64]{1,0:T(8,128)S(1)}, f32[64,64]{1,0:T(8,128)S(1)}, u32[]{:S(2)}, u32[]{:S(2)}) collective-permute-start(f32[64,64]{1,0:T(8,128)S(1)} %add.39), channel_id=1, source_target_pairs={{0,2},{1,3},{2,0},{3,1},{4,6},{5,7},{6,4},{7,5},{8,10},{9,11},{10,... | collective-permute-start | bytes 49160 | tf_op jit(solution)/shard_map/ppermute | solution.py:240
  60.9 5.7 %collective-permute-start.4 = (f32[64,64]{1,0:T(8,128)S(1)}, f32[64,64]{1,0:T(8,128)S(1)}, u32[]{:S(2)}, u32[]{:S(2)}) collective-permute-start(f32[64,64]{1,0:T(8,128)S(1)} %add.40.gram), channel_id=1, source_target_pairs={{0,6},{1,7},{2,4},{3,5},{4,2},{5,3},{6,0},{7,1},{8,14},{9,15},{10,... | collective-permute-start | bytes 49160 | tf_op jit(solution)/shard_map/ppermute | solution.py:240
  72.4 3.8 %collective-permute-start.18 = (f32[64,512]{1,0:T(8,128)S(1)}, f32[64,512]{1,0:T(8,128)S(1)}, u32[]{:S(2)}, u32[]{:S(2)}) collective-permute-start(f32[64,512]{1,0:T(8,128)S(1)} %apply.3.right), channel_id=1, source_target_pairs={{0,8},{1,9},{2,10},{3,11},{4,12},{5,13},{6,14},{7,15},{8,0},{9,1},... | collective-permute-start | bytes 393224 | tf_op jit(solution)/shard_map/ppermute | solution.py:240
  72.7 8.9 %collective-permute-start.12 = (f32[64,512]{1,0:T(8,128)S(1)}, f32[64,512]{1,0:T(8,128)S(1)}, u32[]{:S(2)}, u32[]{:S(2)}) collective-permute-start(f32[64,512]{1,0:T(8,128)S(1)} %apply.2.right), channel_id=1, source_target_pairs={{0,8},{1,9},{2,10},{3,11},{4,12},{5,13},{6,14},{7,15},{8,0},{9,1},... | collective-permute-start | bytes 393224 | tf_op jit(solution)/shard_map/ppermute | solution.py:240
  73.3 2.8 %collective-permute-start.5 = (f32[64,64]{1,0:T(8,128)S(1)}, f32[64,64]{1,0:T(8,128)S(1)}, u32[]{:S(2)}, u32[]{:S(2)}) collective-permute-start(f32[64,64]{1,0:T(8,128)S(1)} %factor.1.inverse), channel_id=1, source_target_pairs={{0,8},{1,9},{2,10},{3,11},{4,12},{5,13},{6,14},{7,15},{8,0},{9,1},... | collective-permute-start | bytes 49160 | tf_op jit(solution)/shard_map/ppermute | solution.py:240

commit v2 on v1

v2 whole, which is shorter than its diff:
```python
import functools

import jax
import jax.numpy as jnp
from jax import lax
from jax.experimental import pallas as pl
from jax.experimental.pallas import tpu as pltpu
from jax.sharding import PartitionSpec as P

AXES = ("rep", "shard")
F32, BF16 = jnp.float32, jnp.bfloat16
HIGHEST = lax.Precision.HIGHEST
NT = (((1,), (1,)), ((), ()))
TN = (((0,), (0,)), ((), ()))
NN = (((1,), (0,)), ((), ()))
LANES = 128
VMEM = pl.BlockSpec(memory_space=pltpu.VMEM)


def dot(a, b, dims, precision=None):
    return lax.dot_general(a, b, dims, precision=precision, preferred_element_type=F32)


def split(x):
    high = x.astype(BF16)
    return high, (x - high.astype(F32)).astype(BF16)


def params(mib, axes=1):
    return pltpu.CompilerParams(
        vmem_limit_bytes=mib << 20, dimension_semantics=("arbitrary",) * axes
    )


def left_kernel(which, grad, error, basis, high, low, left, cut):
    rank = basis.shape[1]

    @pl.when(pl.program_id(0) == 0)
    def _():
        top, rest = split(basis[0])
        cut[:rank] = top
        cut[rank:] = rest

    merged = grad[0, 0].astype(F32) + error[0, 0]
    top, rest = split(merged)
    high[...] = top
    low[...] = rest
    both = dot(cut[...], top, NT)
    left[...] = both[:rank] + both[rank:] + dot(cut[:rank], rest, NT)


def left_of(which, grad, error, basis):
    _, _, rows, cols = grad.shape
    rank = basis.shape[1]
    block = min(rows, 256)
    tile = pl.BlockSpec((1, 1, block, cols), lambda i, w: (0, w[0], i, 0))
    flat = pl.BlockSpec((block, cols), lambda i, w: (i, 0))
    return pl.pallas_call(
        left_kernel,
        name="left",
        grid_spec=pltpu.PrefetchScalarGridSpec(
            num_scalar_prefetch=1,
            grid=(rows // block,),
            in_specs=[tile, tile, pl.BlockSpec((1, rank, cols), lambda i, w: (w[0], 0, 0))],
            out_specs=[flat, flat, pl.BlockSpec((rank, block), lambda i, w: (0, i))],
            scratch_shapes=[pltpu.VMEM((2 * rank, cols), BF16)],
        ),
        out_shape=[
            jax.ShapeDtypeStruct((rows, cols), BF16),
            jax.ShapeDtypeStruct((rows, cols), BF16),
            jax.ShapeDtypeStruct((rank, rows), F32),
        ],
        compiler_params=params(24),
        cost_estimate=pl.CostEstimate(
            flops=6 * rows * cols * rank, bytes_accessed=10 * rows * cols, transcendentals=0
        ),
    )(which, grad, error, basis)


def right_kernel(start, with_gram, left, high, low, right):
    rank = left.shape[0]
    width = right.shape[1] - (LANES if with_gram else 0)
    top, rest = split(left[...])
    columns = slice(start, start + width)
    both = dot(jnp.concatenate([top, rest], axis=0), high[:, columns], NN)
    right[:, :width] = both[:rank] + both[rank:] + dot(top, low[:, columns], NN)
    if with_gram:
        right[:, width:] = jnp.zeros((rank, LANES), F32)
        right[:, width : width + rank] = dot(left[...], left[...], NT, HIGHEST)


def right_of(left, high, low, start, width, with_gram=False):
    rows, cols = high.shape
    rank = left.shape[0]
    return pl.pallas_call(
        functools.partial(right_kernel, start, with_gram),
        name="right",
        in_specs=[VMEM] * 3,
        out_specs=VMEM,
        out_shape=jax.ShapeDtypeStruct((rank, width + (LANES if with_gram else 0)), F32),
        compiler_params=params(16, 0),
        cost_estimate=pl.CostEstimate(
            flops=6 * rows * width * rank, bytes_accessed=4 * rows * width, transcendentals=0
        ),
    )(left, high, low)


def factor_kernel(scale, right_scale, mine, theirs, inverse, right):
    rank = mine.shape[0]
    width = right.shape[1]
    row = lax.broadcasted_iota(jnp.int32, (rank, rank), 0)
    col = lax.broadcasted_iota(jnp.int32, (rank, rank), 1)
    eye = jnp.where(row == col, 1.0, 0.0)
    columns = slice(width, width + rank)
    gram = (mine[:, columns] + theirs[:, columns]) * scale
    work = jnp.concatenate([gram, eye], axis=1)
    below = lax.broadcasted_iota(jnp.int32, (rank, 1), 0)
    for j in range(rank - 1):
        pivot = work[j : j + 1, :]
        scaled = pivot * (1.0 / work[j : j + 1, j : j + 1])
        factor = jnp.where(below > j, work[:, j : j + 1], 0.0)
        work = work - factor * scaled
    diagonal = jnp.sum(work[:, :rank] * eye, axis=1, keepdims=True)
    inverse[...] = work[:, rank:] / jnp.sqrt(diagonal)
    total = (mine[:, :width] + theirs[:, :width]) * right_scale
    right[...] = dot(inverse[...], total, NN, HIGHEST)


def factor_of(mine, theirs, scale, right_scale):
    rank = mine.shape[0]
    width = mine.shape[1] - LANES
    return pl.pallas_call(
        functools.partial(factor_kernel, scale, right_scale),
        name="factor",
        in_specs=[VMEM] * 2,
        out_specs=[VMEM] * 2,
        out_shape=[
            jax.ShapeDtypeStruct((rank, rank), F32),
            jax.ShapeDtypeStruct((rank, width), F32),
        ],
        compiler_params=params(8, 0),
        cost_estimate=pl.CostEstimate(
            flops=4 * rank**3, bytes_accessed=8 * rank * width, transcendentals=rank
        ),
    )(mine, theirs)


def apply_kernel(scale, inverse, mine, theirs, out):
    out[...] = dot(inverse[...], (mine[...] + theirs[...]) * scale, NN, HIGHEST)


def apply_of(inverse, mine, theirs, scale):
    return pl.pallas_call(
        functools.partial(apply_kernel, scale),
        name="apply",
        in_specs=[VMEM] * 3,
        out_specs=VMEM,
        out_shape=jax.ShapeDtypeStruct(mine.shape, F32),
        compiler_params=params(8, 0),
    )(inverse, mine, theirs)


def final_kernel(counts, which, inverse, left, high, low, *refs):
    rights, (update, new_error, basis_next, ortho, pieces) = refs[:counts], refs[-5:]
    rank = left.shape[0]

    @pl.when(pl.program_id(0) == 0)
    def _():
        top, rest = split(dot(left[...], inverse[...], (((0,), (1,)), ((), ())), HIGHEST))
        ortho[:, :rank] = top
        ortho[:, rank : 2 * rank] = top
        ortho[:, 2 * rank :] = rest
        start = 0
        for right in rights:
            columns = slice(start, start + right.shape[1])
            top, rest = split(right[...])
            pieces[:rank, columns] = top
            pieces[rank : 2 * rank, columns] = rest
            pieces[2 * rank :, columns] = top
            basis_next[0, :, columns] = right[...]
            start += right.shape[1]

    block = high.shape[0]
    rows = pl.ds(pl.multiple_of(pl.program_id(0) * block, block), block)
    approx = dot(ortho[rows, :], pieces[...], NN)
    update[0] = approx.astype(BF16)
    new_error[0, 0] = (high[...].astype(F32) + low[...].astype(F32)) - approx


def final_of(which, inverse, left, high, low, rights, outs):
    rows, cols = high.shape
    rank = left.shape[0]
    block = min(rows, 128)
    tile = pl.BlockSpec((block, cols), lambda i, w: (i, 0))
    whole = lambda shape: pl.BlockSpec(shape, lambda i, w: (0, 0))
    return pl.pallas_call(
        functools.partial(final_kernel, len(rights)),
        name="final",
        grid_spec=pltpu.PrefetchScalarGridSpec(
            num_scalar_prefetch=1,
            grid=(rows // block,),
            in_specs=[whole((rank, rank)), whole((rank, rows)), tile, tile]
            + [whole(right.shape) for right in rights]
            + [pl.BlockSpec(memory_space=pl.ANY)] * len(outs),
            out_specs=[
                pl.BlockSpec((1, block, cols), lambda i, w: (w[0], i, 0)),
                pl.BlockSpec((1, 1, block, cols), lambda i, w: (0, w[0], i, 0)),
                pl.BlockSpec((1, rank, cols), lambda i, w: (w[0], 0, 0)),
            ],
            scratch_shapes=[pltpu.VMEM((rows, 3 * rank), BF16), pltpu.VMEM((3 * rank, cols), BF16)],
        ),
        out_shape=[
            jax.ShapeDtypeStruct((2, rows, cols), BF16),
            jax.ShapeDtypeStruct((1, 2, rows, cols), F32),
            jax.ShapeDtypeStruct((2, rank, cols), F32),
        ],
        input_output_aliases={5 + len(rights) + k: k for k in range(len(outs))},
        compiler_params=params(16),
        cost_estimate=pl.CostEstimate(
            flops=6 * rows * cols * rank, bytes_accessed=10 * rows * cols, transcendentals=0
        ),
    )(which, inverse, left, high, low, *rights, *outs)


def bits_of(count):
    return [1 << k for k in range(count.bit_length() - 1)]


def on_device(replicas, shards, grad_kv, error_kv, basis_kv):
    def swap(value, *masks):
        pairs = []
        for r in range(replicas):
            for s in range(shards):
                rep_mask, shard_mask = masks[r % len(masks)]
                pairs.append((r * shards + s, (r ^ rep_mask) * shards + (s ^ shard_mask)))
        return lax.ppermute(value, AXES, pairs)

    def core(value):
        return swap(value, (1, 0))

    rep_steps = [(mask, 0) for mask in bits_of(replicas)[1:]]
    masks = bits_of(shards)
    masks[-1] |= masks[-2]
    steps = rep_steps + [(0, mask) for mask in masks]
    scale = 1.0 / replicas

    def order(part):
        turns = [steps[turn:] + steps[:turn] for turn in (2 * part, 2 * part + 1)]
        return list(zip(*turns))

    grad_kv, error_kv = (pltpu.with_memory_space_constraint(x, pltpu.HBM) for x in (grad_kv, error_kv))
    basis = basis_kv.transpose(0, 2, 1)
    mine = (lax.axis_index("rep") % 2).astype(jnp.int32).reshape(1)
    theirs = 1 - mine

    high_t, low_t, left_t = left_of(theirs, grad_kv, error_kv, basis)
    arriving = core(left_t)
    high_m, low_m, left_m = left_of(mine, grad_kv, error_kv, basis)
    left_m = left_m + arriving
    for step in rep_steps:
        left_m = left_m + swap(left_m, step)
    left_m = left_m * scale
    left_t = core(left_m)

    cols = high_m.shape[1]
    first = cols * 3 // 8
    pieces = ((0, first), (first, cols - first))
    sums = []
    for part, (start, width) in enumerate(pieces):
        right_t = core(right_of(left_t, high_t, low_t, start, width))
        right = right_of(left_m, high_m, low_m, start, width, part == 0)
        right = right + jnp.pad(right_t, ((0, 0), (0, right.shape[1] - width)))
        *early, last = order(part)
        for step in early:
            right = right + swap(right, *step)
        sums.append((right, swap(right, *last)))

    inverse_m, right_a = factor_of(*sums[0], 2.0 / replicas, scale)
    right_b = apply_of(inverse_m, *sums[1], scale)
    rights_m = (right_a, right_b)
    inverse_t = core(inverse_m)
    rights_t = tuple(core(right) for right in rights_m)

    outs = final_of(mine, inverse_m, left_m, high_m, low_m, rights_m, ())
    outs = final_of(theirs, inverse_t, left_t, high_t, low_t, rights_t, outs)
    update, new_error, right = outs
    return update, new_error, right.transpose(0, 2, 1)


def solution(mesh):
    placed = (P("rep", None, "shard", None), P("rep", None, "shard", None), P())
    return jax.shard_map(
        functools.partial(on_device, mesh.shape["rep"], mesh.shape["shard"]),
        mesh=mesh,
        in_specs=placed,
        out_specs=(P(None, "shard", None), P("rep", None, "shard", None), P()),
        check_vma=False,
    )
```

time: 84.7 us -> 73.2 us (0.86)
  local copies, waits for them, and re-layouts: 8.64 us -> 1.04 us
  starting transfers between devices: 26.1 us -> 18.9 us
  Pallas kernels: 25.1 us -> 28 us
    unnamed x10 -> x4, local copies, waits for them, and re-layouts: 8.64 us -> 1.04 us
    ppermute x19 -> x16, starting transfers between devices: 26.1 us -> 18.9 us  [swap(): return lax.ppermute(value, AXES, pairs)]
    pallas_call x2, Pallas kernels: 3.94 us -> 8.86 us  [left_of(): pl.pallas_call(left_kernel, name='left', grid_spec=pltpu.PrefetchScalarGr...]
    pallas_call x12 -> x8, Pallas kernels: 21.2 us -> 19.2 us  [the longest x2 10.9 us: final_of(): pl.pallas_call(functools.partial(final_kernel, len(rights)), name='final'...]
    ppermute x19 -> x16, waiting for transfers between devices: 23.5 us -> 24 us  [swap(): return lax.ppermute(value, AXES, pairs)]
  transfers between devices with their start and end apart: 19 -> 16, of which waited for: 10 -> 8; matrix products, arithmetic and copies ran while one was open for 0% -> 0% of each run, Pallas kernels for 23% -> 23%
where the time goes in v2:
time: 73.2 us; the launch traced here: 73 us
  Pallas kernels  28 us (38%)
  waiting for transfers between devices  24 us (33%)
  starting transfers between devices  18.9 us (26%)
  local copies, waits for them, and re-layouts  1.04 us (1%)
  between operations  0.81 us (1%)
    ppermute x16, waiting for transfers between devices, swap(): return lax.ppermute(value, AXES, pairs)  24 us
    ppermute x16, starting transfers between devices, swap(): return lax.ppermute(value, AXES, pairs)  18.9 us
    pallas_call x2, Pallas kernels, final_of(): pl.pallas_call(functools.partial(final_kernel, len(rights)), name='final'...  10.9 us
    pallas_call x2, Pallas kernels, left_of(): pl.pallas_call(left_kernel, name='left', grid_spec=pltpu.PrefetchScalarGr...  8.86 us
    pallas_call x1, Pallas kernels, factor_of(): pl.pallas_call(functools.partial(factor_kernel, scale, right_scale), name...  5.68 us
    pallas_call x4, Pallas kernels, right_of(): pl.pallas_call(functools.partial(right_kernel, start, with_gram), name='r...  2.25 us
  transfers between devices with their start and end apart: 16, of which 8 were waited for; matrix products, arithmetic and copies ran while one was open for 0% of the time, Pallas kernels for 23%

profile of v2, /device:TPU:0, one launch (start us, length us, event | category | flops | bytes accessed | tf_op | source)
XLA Modules:
  0.0 73.0 jit_solution(4163208694244822896)
XLA Ops:
  0.6 0.0 copy-start
  0.7 1.0 %copy-done = f32[2,1024,64]{1,2,0:T(8,128)S(1)} copy-done((f32[2,1024,64]{1,2,0:T(8,128)S(1)}, f32[2,1024,64]{1,2,0:T(8,128)}, u32[]{:S(2)}) %copy-start) | copy-done | bytes 524312
  1.7 0.0 copy-start.1
  1.7 4.5 %left.3 = (bf16[1024,1024]{1,0:T(8,128)(2,1)S(1)}, bf16[1024,1024]{1,0:T(8,128)(2,1)S(1)}, f32[64,1024]{1,0:T(8,128)S(1)}) custom-call(s32[1]{0:T(128)S(6)} %sub.3.which, bf16[1,2,1024,1024]{3,2,1,0:T(8,128)(2,1)} %grad.3, f32[1,2,1024,1024]{3,2,1,0:T(8,128)} %error.3, f32[2,64,1024]{2,1,0:T(8,128)S(1)} %bitcast.3), custom_call_target="tpu_custom_call" | custom-call | flops 402653184 | bytes 10485760 | tf_op jit(solution)/shard_map/left/pallas_call | solution.py:58
  6.2 0.6 collective-permute-start
  6.7 0.0 copy-done.1
  6.7 4.4 %left.2 = (bf16[1024,1024]{1,0:T(8,128)(2,1)S(1)}, bf16[1024,1024]{1,0:T(8,128)(2,1)S(1)}, f32[64,1024]{1,0:T(8,128)S(1)}) custom-call(s32[1]{0:T(128)} %bitcast.which, bf16[1,2,1024,1024]{3,2,1,0:T(8,128)(2,1)} %grad.3, f32[1,2,1024,1024]{3,2,1,0:T(8,128)} %error.3, f32[2,64,1024]{2,1,0:T(8,128)S(1)} %bitcast.4), custom_call_target="tpu_custom_call" | custom-call | flops 402653184 | bytes 10485760 | tf_op jit(solution)/shard_map/left/pallas_call | solution.py:58
  11.1 0.0 collective-permute-done
  11.2 2.6 %collective-permute-start.1 = (f32[64,1024]{1,0:T(8,128)S(1)}, f32[64,1024]{1,0:T(8,128)S(1)}, u32[]{:S(2)}, u32[]{:S(2)}) collective-permute-start(f32[64,1024]{1,0:T(8,128)S(1)} %add.37), channel_id=1, source_target_pairs={{0,16},{1,17},{2,18},{3,19},{4,20},{5,21},{6,22},{7,23},{8,24},{9,... | collective-permute-start | bytes 786440 | tf_op jit(solution)/shard_map/ppermute | solution.py:236
  13.8 6.9 %collective-permute-done.1 = f32[64,1024]{1,0:T(8,128)S(1)} collective-permute-done((f32[64,1024]{1,0:T(8,128)S(1)}, f32[64,1024]{1,0:T(8,128)S(1)}, u32[]{:S(2)}, u32[]{:S(2)}) %collective-permute-start.1) | collective-permute-done | bytes 262176 | tf_op jit(solution)/shard_map/ppermute | solution.py:236
  20.8 0.1 collective-permute-start.2
  20.8 1.5 %collective-permute-done.2.left = f32[64,1024]{1,0:T(8,128)S(1)} collective-permute-done((f32[64,1024]{1,0:T(8,128)S(1)}, f32[64,1024]{1,0:T(8,128)S(1)}, u32[]{:S(2)}, u32[]{:S(2)}) %collective-permute-start.2) | collective-permute-done | bytes 262176 | tf_op jit(solution)/shard_map/ppermute | solution.py:236
  22.4 0.6 right.7
  23.0 0.2 collective-permute-start.10
  23.2 0.4 right.5
  23.6 0.4 collective-permute-start.3
  24.0 0.6 right.4
  24.6 0.6 right.6
  25.3 0.0 collective-permute-done.10
  25.3 1.9 %collective-permute-start.11 = (f32[64,640]{1,0:T(8,128)S(1)}, f32[64,640]{1,0:T(8,128)S(1)}, u32[]{:S(2)}, u32[]{:S(2)}) collective-permute-start(f32[64,640]{1,0:T(8,128)S(1)} %add.43), channel_id=1, source_target_pairs={{0,2},{1,3},{2,0},{3,1},{4,6},{5,7},{6,4},{7,5},{8,14},{9,15},{10,... | collective-permute-start | bytes 491528 | tf_op jit(solution)/shard_map/ppermute | solution.py:236
  27.2 0.0 collective-permute-done.3
  27.2 1.6 %collective-permute-start.4 = (f32[64,512]{1,0:T(8,128)S(1)}, f32[64,512]{1,0:T(8,128)S(1)}, u32[]{:S(2)}, u32[]{:S(2)}) collective-permute-start(f32[64,512]{1,0:T(8,128)S(1)} %pad_add_fusion), channel_id=1, source_target_pairs={{0,16},{1,17},{2,18},{3,19},{4,20},{5,21},{6,22},{7,23},{8,9},{9,8... | collective-permute-start | bytes 393224 | tf_op jit(solution)/shard_map/ppermute | solution.py:236
  28.8 3.3 %collective-permute-done.11 = f32[64,640]{1,0:T(8,128)S(1)} collective-permute-done((f32[64,640]{1,0:T(8,128)S(1)}, f32[64,640]{1,0:T(8,128)S(1)}, u32[]{:S(2)}, u32[]{:S(2)}) %collective-permute-start.11) | collective-permute-done | bytes 163872 | tf_op jit(solution)/shard_map/ppermute | solution.py:236
  32.1 4.2 %collective-permute-start.12 = (f32[64,640]{1,0:T(8,128)S(1)}, f32[64,640]{1,0:T(8,128)S(1)}, u32[]{:S(2)}, u32[]{:S(2)}) collective-permute-start(f32[64,640]{1,0:T(8,128)S(1)} %add.44), channel_id=1, source_target_pairs={{0,6},{1,7},{2,4},{3,5},{4,2},{5,3},{6,0},{7,1},{8,24},{9,25},{10,... | collective-permute-start | bytes 491528 | tf_op jit(solution)/shard_map/ppermute | solution.py:236
  36.4 0.0 collective-permute-done.4
  36.4 1.6 %collective-permute-start.5 = (f32[64,512]{1,0:T(8,128)S(1)}, f32[64,512]{1,0:T(8,128)S(1)}, u32[]{:S(2)}, u32[]{:S(2)}) collective-permute-start(f32[64,512]{1,0:T(8,128)S(1)} %add.40), channel_id=1, source_target_pairs={{0,1},{1,0},{2,3},{3,2},{4,5},{5,4},{6,7},{7,6},{8,10},{9,11},{10,... | collective-permute-start | bytes 393224 | tf_op jit(solution)/shard_map/ppermute | solution.py:236
  37.9 3.1 %collective-permute-done.12 = f32[64,640]{1,0:T(8,128)S(1)} collective-permute-done((f32[64,640]{1,0:T(8,128)S(1)}, f32[64,640]{1,0:T(8,128)S(1)}, u32[]{:S(2)}, u32[]{:S(2)}) %collective-permute-start.12) | collective-permute-done | bytes 163872 | tf_op jit(solution)/shard_map/ppermute | solution.py:236
  41.1 0.9 %collective-permute-start.13 = (f32[64,640]{1,0:T(8,128)S(1)}, f32[64,640]{1,0:T(8,128)S(1)}, u32[]{:S(2)}, u32[]{:S(2)}) collective-permute-start(f32[64,640]{1,0:T(8,128)S(1)} %add.45), channel_id=1, source_target_pairs={{0,16},{1,17},{2,18},{3,19},{4,20},{5,21},{6,22},{7,23},{8,9},{9,8... | collective-permute-start | bytes 491528 | tf_op jit(solution)/shard_map/ppermute | solution.py:236
  42.0 0.7 collective-permute-done.5
  42.7 0.1 collective-permute-start.6
  42.8 3.7 %collective-permute-done.13 = f32[64,640]{1,0:T(8,128)S(1)} collective-permute-done((f32[64,640]{1,0:T(8,128)S(1)}, f32[64,640]{1,0:T(8,128)S(1)}, u32[]{:S(2)}, u32[]{:S(2)}) %collective-permute-start.13) | collective-permute-done | bytes 163872 | tf_op jit(solution)/shard_map/ppermute | solution.py:236
  46.5 1.7 %collective-permute-start.14 = (f32[64,640]{1,0:T(8,128)S(1)}, f32[64,640]{1,0:T(8,128)S(1)}, u32[]{:S(2)}, u32[]{:S(2)}) collective-permute-start(f32[64,640]{1,0:T(8,128)S(1)} %add.46.mine), channel_id=1, source_target_pairs={{0,1},{1,0},{2,3},{3,2},{4,5},{5,4},{6,7},{7,6},{8,10},{9,11},{10,... | collective-permute-start | bytes 491528 | tf_op jit(solution)/shard_map/ppermute | solution.py:236
  48.1 0.3 collective-permute-done.6
  48.5 2.5 %collective-permute-start.7 = (f32[64,512]{1,0:T(8,128)S(1)}, f32[64,512]{1,0:T(8,128)S(1)}, u32[]{:S(2)}, u32[]{:S(2)}) collective-permute-start(f32[64,512]{1,0:T(8,128)S(1)} %add.42.mine), channel_id=1, source_target_pairs={{0,6},{1,7},{2,4},{3,5},{4,2},{5,3},{6,0},{7,1},{8,24},{9,25},{10,... | collective-permute-start | bytes 393224 | tf_op jit(solution)/shard_map/ppermute | solution.py:236
  51.0 4.3 %collective-permute-done.7.theirs = f32[64,512]{1,0:T(8,128)S(1)} collective-permute-done((f32[64,512]{1,0:T(8,128)S(1)}, f32[64,512]{1,0:T(8,128)S(1)}, u32[]{:S(2)}, u32[]{:S(2)}) %collective-permute-start.7) | collective-permute-done | bytes 131104 | tf_op jit(solution)/shard_map/ppermute | solution.py:236
  55.4 5.7 %factor.1 = (f32[64,64]{1,0:T(8,128)S(1)}, f32[64,384]{1,0:T(8,128)S(1)}) custom-call(f32[64,512]{1,0:T(8,128)S(1)} %add.42.mine, f32[64,512]{1,0:T(8,128)S(1)} %collective-permute-done.7.theirs), custom_call_target="tpu_custom_call" | custom-call | flops 1048576 | bytes 196608 | tf_op jit(solution)/shard_map/factor/pallas_call | solution.py:132
  61.0 0.0 collective-permute-done.14.theirs
  61.1 0.3 apply.1.refs_1_
  61.3 0.1 collective-permute-start.15
  61.4 0.5 collective-permute-start.9
  61.9 0.1 collective-permute-start.8
  62.0 5.4 %final.2 = (bf16[2,1024,1024]{2,1,0:T(8,128)(2,1)}, f32[1,2,1024,1024]{3,2,1,0:T(8,128)}, f32[2,64,1024]{2,1,0:T(8,128)}) custom-call(s32[1]{0:T(128)} %bitcast.which, f32[64,64]{1,0:T(8,128)S(1)} %get-tuple-element.23.inverse, f32[64,1024]{1,0:T(8,128)S(1)} %add_multiply_fusion.left, bf16[1024,1024]{1,0:T(8,128)(2,1)S(1)} %get-tuple-element.19.high, ...), custom_call_target="tpu_custom_call" | custom-call | flops 402653184 | bytes 10485760 | tf_op jit(solution)/shard_map/final/pallas_call | solution.py:196
  67.4 0.0 collective-permute-done.8.inverse
  67.4 0.0 collective-permute-done.9.refs_0_
  67.4 0.0 collective-permute-done.15.refs_1_
  67.5 5.5 %final.3 = (bf16[2,1024,1024]{2,1,0:T(8,128)(2,1)}, f32[1,2,1024,1024]{3,2,1,0:T(8,128)}, f32[2,64,1024]{2,1,0:T(8,128)}) custom-call(s32[1]{0:T(128)S(6)} %sub.3.which, f32[64,64]{1,0:T(8,128)S(1)} %collective-permute-done.8.inverse, f32[64,1024]{1,0:T(8,128)S(1)} %collective-permute-done.2.left, ...), custom_call_target="tpu_custom_call", output_to_operand_aliasing={{0}: (7, {}), {1}: (8, {}), {2}: (9, {})} | custom-call | flops 402653184 | bytes 10485760 | tf_op jit(solution)/shard_map/final/pallas_call | solution.py:196
  (10 shorter events, 0.2 us)
Async XLA Ops:
  0.6 1.0 %copy-start = (f32[2,1024,64]{1,2,0:T(8,128)S(1)}, f32[2,1024,64]{1,2,0:T(8,128)}, u32[]{:S(2)}) copy-start(f32[2,1024,64]{1,2,0:T(8,128)} %param.5) | copy-start | bytes 1572868
  1.7 5.0 %copy-start.1 = (f32[2,1024,64]{1,2,0:T(8,128)S(1)}, f32[2,1024,64]{1,2,0:T(8,128)}, u32[]{:S(2)}) copy-start(f32[2,1024,64]{1,2,0:T(8,128)} %param.5) | copy-start | bytes 1572868
  6.2 5.0 %collective-permute-start = (f32[64,1024]{1,0:T(8,128)S(1)}, f32[64,1024]{1,0:T(8,128)S(1)}, u32[]{:S(2)}, u32[]{:S(2)}) collective-permute-start(f32[64,1024]{1,0:T(8,128)S(1)} %get-tuple-element.18), channel_id=1, source_target_pairs={{0,8},{1,9},{2,10},{3,11},{4,12},{5,13},{6,14},{7,15},{8,0},{9,1},... | collective-permute-start | bytes 786440 | tf_op jit(solution)/shard_map/ppermute | solution.py:236
  11.2 9.5 %collective-permute-start.1 = (f32[64,1024]{1,0:T(8,128)S(1)}, f32[64,1024]{1,0:T(8,128)S(1)}, u32[]{:S(2)}, u32[]{:S(2)}) collective-permute-start(f32[64,1024]{1,0:T(8,128)S(1)} %add.37), channel_id=1, source_target_pairs={{0,16},{1,17},{2,18},{3,19},{4,20},{5,21},{6,22},{7,23},{8,24},{9,... | collective-permute-start | bytes 786440 | tf_op jit(solution)/shard_map/ppermute | solution.py:236
  20.8 1.6 %collective-permute-start.2 = (f32[64,1024]{1,0:T(8,128)S(1)}, f32[64,1024]{1,0:T(8,128)S(1)}, u32[]{:S(2)}, u32[]{:S(2)}) collective-permute-start(f32[64,1024]{1,0:T(8,128)S(1)} %add_multiply_fusion.left), channel_id=1, source_target_pairs={{0,8},{1,9},{2,10},{3,11},{4,12},{5,13},{6,14},{7,15},{8,0},{9,1},... | collective-permute-start | bytes 786440 | tf_op jit(solution)/shard_map/ppermute | solution.py:236
  23.0 2.3 %collective-permute-start.10 = (f32[64,640]{1,0:T(8,128)S(1)}, f32[64,640]{1,0:T(8,128)S(1)}, u32[]{:S(2)}, u32[]{:S(2)}) collective-permute-start(f32[64,640]{1,0:T(8,128)S(1)} %right.7), channel_id=1, source_target_pairs={{0,8},{1,9},{2,10},{3,11},{4,12},{5,13},{6,14},{7,15},{8,0},{9,1},... | collective-permute-start | bytes 491528 | tf_op jit(solution)/shard_map/ppermute | solution.py:236
  23.6 3.6 %collective-permute-start.3 = (f32[64,384]{1,0:T(8,128)S(1)}, f32[64,384]{1,0:T(8,128)S(1)}, u32[]{:S(2)}, u32[]{:S(2)}) collective-permute-start(f32[64,384]{1,0:T(8,128)S(1)} %right.5), channel_id=1, source_target_pairs={{0,8},{1,9},{2,10},{3,11},{4,12},{5,13},{6,14},{7,15},{8,0},{9,1},... | collective-permute-start | bytes 294920 | tf_op jit(solution)/shard_map/ppermute | solution.py:236
  25.3 6.8 %collective-permute-start.11 = (f32[64,640]{1,0:T(8,128)S(1)}, f32[64,640]{1,0:T(8,128)S(1)}, u32[]{:S(2)}, u32[]{:S(2)}) collective-permute-start(f32[64,640]{1,0:T(8,128)S(1)} %add.43), channel_id=1, source_target_pairs={{0,2},{1,3},{2,0},{3,1},{4,6},{5,7},{6,4},{7,5},{8,14},{9,15},{10,... | collective-permute-start | bytes 491528 | tf_op jit(solution)/shard_map/ppermute | solution.py:236
  27.2 9.2 %collective-permute-start.4 = (f32[64,512]{1,0:T(8,128)S(1)}, f32[64,512]{1,0:T(8,128)S(1)}, u32[]{:S(2)}, u32[]{:S(2)}) collective-permute-start(f32[64,512]{1,0:T(8,128)S(1)} %pad_add_fusion), channel_id=1, source_target_pairs={{0,16},{1,17},{2,18},{3,19},{4,20},{5,21},{6,22},{7,23},{8,9},{9,8... | collective-permute-start | bytes 393224 | tf_op jit(solution)/shard_map/ppermute | solution.py:236
  32.1 8.9 %collective-permute-start.12 = (f32[64,640]{1,0:T(8,128)S(1)}, f32[64,640]{1,0:T(8,128)S(1)}, u32[]{:S(2)}, u32[]{:S(2)}) collective-permute-start(f32[64,640]{1,0:T(8,128)S(1)} %add.44), channel_id=1, source_target_pairs={{0,6},{1,7},{2,4},{3,5},{4,2},{5,3},{6,0},{7,1},{8,24},{9,25},{10,... | collective-permute-start | bytes 491528 | tf_op jit(solution)/shard_map/ppermute | solution.py:236
  36.4 6.3 %collective-permute-start.5 = (f32[64,512]{1,0:T(8,128)S(1)}, f32[64,512]{1,0:T(8,128)S(1)}, u32[]{:S(2)}, u32[]{:S(2)}) collective-permute-start(f32[64,512]{1,0:T(8,128)S(1)} %add.40), channel_id=1, source_target_pairs={{0,1},{1,0},{2,3},{3,2},{4,5},{5,4},{6,7},{7,6},{8,10},{9,11},{10,... | collective-permute-start | bytes 393224 | tf_op jit(solution)/shard_map/ppermute | solution.py:236
  41.1 5.4 %collective-permute-start.13 = (f32[64,640]{1,0:T(8,128)S(1)}, f32[64,640]{1,0:T(8,128)S(1)}, u32[]{:S(2)}, u32[]{:S(2)}) collective-permute-start(f32[64,640]{1,0:T(8,128)S(1)} %add.45), channel_id=1, source_target_pairs={{0,16},{1,17},{2,18},{3,19},{4,20},{5,21},{6,22},{7,23},{8,9},{9,8... | collective-permute-start | bytes 491528 | tf_op jit(solution)/shard_map/ppermute | solution.py:236
  42.7 5.8 %collective-permute-start.6 = (f32[64,512]{1,0:T(8,128)S(1)}, f32[64,512]{1,0:T(8,128)S(1)}, u32[]{:S(2)}, u32[]{:S(2)}) collective-permute-start(f32[64,512]{1,0:T(8,128)S(1)} %add.41), channel_id=1, source_target_pairs={{0,2},{1,3},{2,0},{3,1},{4,6},{5,7},{6,4},{7,5},{8,14},{9,15},{10,... | collective-permute-start | bytes 393224 | tf_op jit(solution)/shard_map/ppermute | solution.py:236
  46.5 14.6 %collective-permute-start.14 = (f32[64,640]{1,0:T(8,128)S(1)}, f32[64,640]{1,0:T(8,128)S(1)}, u32[]{:S(2)}, u32[]{:S(2)}) collective-permute-start(f32[64,640]{1,0:T(8,128)S(1)} %add.46.mine), channel_id=1, source_target_pairs={{0,1},{1,0},{2,3},{3,2},{4,5},{5,4},{6,7},{7,6},{8,10},{9,11},{10,... | collective-permute-start | bytes 491528 | tf_op jit(solution)/shard_map/ppermute | solution.py:236
  48.5 6.8 %collective-permute-start.7 = (f32[64,512]{1,0:T(8,128)S(1)}, f32[64,512]{1,0:T(8,128)S(1)}, u32[]{:S(2)}, u32[]{:S(2)}) collective-permute-start(f32[64,512]{1,0:T(8,128)S(1)} %add.42.mine), channel_id=1, source_target_pairs={{0,6},{1,7},{2,4},{3,5},{4,2},{5,3},{6,0},{7,1},{8,24},{9,25},{10,... | collective-permute-start | bytes 393224 | tf_op jit(solution)/shard_map/ppermute | solution.py:236
  61.3 6.1 %collective-permute-start.15 = (f32[64,640]{1,0:T(8,128)S(1)}, f32[64,640]{1,0:T(8,128)S(1)}, u32[]{:S(2)}, u32[]{:S(2)}) collective-permute-start(f32[64,640]{1,0:T(8,128)S(1)} %apply.1.refs_1_), channel_id=1, source_target_pairs={{0,8},{1,9},{2,10},{3,11},{4,12},{5,13},{6,14},{7,15},{8,0},{9,1},... | collective-permute-start | bytes 491528 | tf_op jit(solution)/shard_map/ppermute | solution.py:236
  61.4 6.0 %collective-permute-start.9 = (f32[64,384]{1,0:T(8,128)S(1)}, f32[64,384]{1,0:T(8,128)S(1)}, u32[]{:S(2)}, u32[]{:S(2)}) collective-permute-start(f32[64,384]{1,0:T(8,128)S(1)} %get-tuple-element.24.refs_0_), channel_id=1, source_target_pairs={{0,8},{1,9},{2,10},{3,11},{4,12},{5,13},{6,14},{7,15},{8,0},{9,1},... | collective-permute-start | bytes 294920 | tf_op jit(solution)/shard_map/ppermute | solution.py:236
  61.9 5.5 %collective-permute-start.8 = (f32[64,64]{1,0:T(8,128)S(1)}, f32[64,64]{1,0:T(8,128)S(1)}, u32[]{:S(2)}, u32[]{:S(2)}) collective-permute-start(f32[64,64]{1,0:T(8,128)S(1)} %get-tuple-element.23.inverse), channel_id=1, source_target_pairs={{0,8},{1,9},{2,10},{3,11},{4,12},{5,13},{6,14},{7,15},{8,0},{9,1},... | collective-permute-start | bytes 49160 | tf_op jit(solution)/shard_map/ppermute | solution.py:236
